TPU v7x, 128 devices: a whole 4x4x4 slice. The times are simulated.
128 devices in a mesh: rep: 16 (over y_hi, x, core), shard: 8 (over z, y_lo).
Axes of the slice: x: 4, y: 4 (y_hi: 2, y_lo: 2; y = y_hi * 2 + y_lo), z: 4, core: 2. Of those that a mesh axis runs over, the one named last changes fastest.
Arguments:
- layer_in: float32 [32768, 1024], P(('rep', 'shard')), may hold values from -6 to 6
- cotangent: float32 [32768, 1024], P(('rep', 'shard')), may hold values from -6 to 6
- seq_lengths: int32 [128, 2], P(('rep', 'shard')), may hold values from 1 to 192, 256 in all within a row
- norm_gain: float32 [1024], P('shard'), may hold values from 0.5 to 1.5
- in_weight: bfloat16 [1024, 4384], P('shard'), may hold values from -0.1875 to 0.1875
- conv_weight: float32 [2304, 4], P('shard'), may hold values from -3 to 3
- conv_bias: float32 [2304], P('shard'), may hold values from -0.5 to 0.5
- step_bias: float32 [32], P('shard'), may hold values from -6.9 to -2.3
- decay_log: float32 [32], P('shard'), may hold values from 0 to 2.77
- skip_gain: float32 [32], P('shard'), may hold values from 0.5 to 1.5
- gate_gain: float32 [2048], P('shard'), may hold values from 0.5 to 1.5
- out_weight: bfloat16 [2048, 1024], P('shard'), may hold values from -0.125 to 0.125
Outputs:
- layer_out: float32 [32768, 1024], P(('rep', 'shard'))
- input_grad: float32 [32768, 1024], P(('rep', 'shard'))
- norm_gain_grad: float32 [1024], P('shard')
- in_weight_grad: float32 [1024, 4384], P('shard')
- conv_weight_grad: float32 [2304, 4], P('shard')
- conv_bias_grad: float32 [2304], P('shard')
- step_bias_grad: float32 [32], P('shard')
- decay_log_grad: float32 [32], P('shard')
- skip_gain_grad: float32 [32], P('shard')
- gate_gain_grad: float32 [2048], P('shard')
- out_weight_grad: float32 [2048, 1024], P('shard')
Inputs may be any that keep to these rules, and one draw needn't show every extreme that they name: `seq_lengths`: each device's row of 2 lengths sums to 256.
All inputs are finite; a program needn't handle non-finite values.
Results may differ from a plain program's by a relative error of at most 0.0064.
Values may be sent and summed in bfloat16 or wider, within the bound.
No kernel may reach another device: no remote copies, remote signals or barrier semaphores. Data moves between devices by JAX's collectives and lax.ppermute only.
A program may use at most 128 MiB of HBM per device.

v0:
```python
import math
import jax
import jax.numpy as jnp
from jax import lax
from jax.sharding import Mesh
from jax.sharding import PartitionSpec as P

SPAN = 256
SHARD = ("shard_0", "shard_1")
REP = ("rep_hi", "core")
REP_SHARD = ("rep_hi", "core", "shard_0", "shard_1")
ALL = REP_SHARD
EPS = 1e-05
HIGH = lax.Precision.HIGHEST


def side_by_side(arrays, axis, dim, along):
    widths = [math.prod(a.shape[along:]) for a in arrays]
    both = jnp.concatenate(
        [a.reshape(*a.shape[:along], w) for a, w in zip(arrays, widths)], axis=along
    )
    result = lax.all_gather(both, axis, axis=dim, tiled=True)
    blocks = jnp.split(result, [sum(widths[:k]) for k in range(1, len(widths))], axis=along)
    return tuple(
        (b.reshape(*result.shape[:along], *a.shape[along:]) for a, b in zip(arrays, blocks))
    )


def sum_by_axis(total, axes):
    for axis in axes:
        total = lax.psum_scatter(total, axis, scatter_dimension=0, tiled=True)
    return total


def in_blocks(shard, dim, size):
    before, after = (shard.shape[:dim], shard.shape[dim + 1 :])
    return jnp.moveaxis(shard.reshape(*before, size, -1, *after), dim, 0)


def sum_at_owner(shard, axis, dim):
    size = lax.axis_size(axis)
    blocks = lax.all_to_all(in_blocks(shard, dim, size), axis, 0, 0, tiled=True)
    return jnp.sum(blocks, axis=0)


def sent_together(arrays, axis, dim, along):
    widths = [math.prod(a.shape[along:]) for a in arrays]
    both = jnp.concatenate(
        [a.reshape(*a.shape[:along], w) for a, w in zip(arrays, widths)], axis=along
    )
    result = sum_at_owner(both, axis, dim)
    blocks = jnp.split(result, [sum(widths[:k]) for k in range(1, len(widths))], axis=along)
    return tuple(
        (b.reshape(*result.shape[:along], *a.shape[along:]) for a, b in zip(arrays, blocks))
    )


def shifted(values, lag):
    zeros_top = jnp.zeros((lag,) + values.shape[1:], values.dtype)
    return jnp.concatenate([zeros_top, values[:-lag]], axis=0)


def segment_ids(lengths_row, count):
    offsets = jnp.cumsum(lengths_row, dtype=jnp.int32) - lengths_row
    places = jnp.arange(count, dtype=jnp.int32)
    return (
        jnp.sum((places[:, None] >= offsets[None, :]).astype(jnp.int32), axis=1, dtype=jnp.int32)
        - 1
    )


def row_product(left, right):
    return lax.dot_general(
        left, right, (((0,), (0,)), ((), ())), preferred_element_type=jnp.float32
    )


def back_product(left, right):
    return lax.dot_general(
        left, right, (((1,), (1,)), ((), ())), preferred_element_type=jnp.float32
    )


def norm_input(inputs, gain_one):
    scaling = lax.rsqrt(jnp.mean(inputs * inputs, axis=1, keepdims=True) + EPS)
    return inputs * scaling * gain_one[None, :]


def mixer(projected, segment, conv_weight, conv_bias, step_bias, decay_log, skip_gain, gate_gain):
    count = projected.shape[0]
    inner = gate_gain.shape[0]
    heads = step_bias.shape[0]
    head_dim = inner // heads
    channels = conv_weight.shape[0]
    state_dim = (channels - inner) // 2
    taps = conv_weight.shape[1]
    gate_part = projected[:, :inner]
    conv_in = projected[:, inner : inner + channels]
    step_raw = projected[:, inner + channels :]
    places = jnp.arange(count, dtype=jnp.int32)
    conv_out = conv_bias[None, :] + conv_weight[:, taps - 1][None, :] * conv_in
    for lag in range(1, taps):
        same = (shifted(segment, lag) == segment) & (places >= lag)
        conv_out = conv_out + jnp.where(
            same[:, None], conv_weight[:, taps - 1 - lag][None, :] * shifted(conv_in, lag), 0.0
        )
    activated = jax.nn.silu(conv_out)
    values = activated[:, :inner].reshape(count, heads, head_dim)
    b_matrix = activated[:, inner : inner + state_dim]
    c_matrix = activated[:, inner + state_dim :]
    step_size = jax.nn.softplus(step_raw + step_bias[None, :])
    decay = -jnp.exp(decay_log)[None, :] * step_size
    blocks = count // SPAN
    values_c = values.reshape(blocks, SPAN, heads, head_dim)
    b_spans = b_matrix.reshape(blocks, SPAN, state_dim)
    c_spans = c_matrix.reshape(blocks, SPAN, state_dim)
    step_c = step_size.reshape(blocks, SPAN, heads)
    cumul = jnp.cumsum(decay.reshape(blocks, SPAN, heads), axis=1)
    seg_c = segment.reshape(blocks, SPAN)
    rows_in = jnp.arange(SPAN, dtype=jnp.int32)
    lower = rows_in[:, None] >= rows_in[None, :]
    allowed = lower[None] & (seg_c[:, :, None] == seg_c[:, None, :])
    cumul_t = jnp.transpose(cumul, (0, 2, 1))
    differ = cumul_t[:, :, :, None] - cumul_t[:, :, None, :]
    weights_l = jnp.exp(jnp.where(allowed[:, None], differ, -10000.0))
    scores = jnp.einsum("cin,cjn->cij", c_spans, b_spans, precision=HIGH)
    mixing = weights_l * scores[:, None]
    scaled_in = values_c * step_c[..., None]
    y_intra = jnp.einsum("chij,cjhp->cihp", mixing, scaled_in, precision=HIGH)
    carried = jnp.zeros((heads, head_dim, state_dim), jnp.float32)
    before_seg = jnp.int32(-1)
    linked = (seg_c[0] == before_seg).astype(jnp.float32)
    reach = jnp.exp(cumul[0]) * linked[:, None]
    inter = jnp.einsum("in,hpn->ihp", c_spans[0], carried, precision=HIGH) * reach[:, :, None]
    pieces = [y_intra[0] + inter]
    y_all = jnp.concatenate(pieces, axis=0) + skip_gain[None, :, None] * values
    gated_pre = y_all.reshape(count, inner) * jax.nn.silu(gate_part)
    scaling = lax.rsqrt(jnp.mean(gated_pre * gated_pre, axis=1, keepdims=True) + EPS)
    return gated_pre * scaling * gate_gain[None, :]


def gather_rows(weight):
    rows = weight.shape[0]
    half = rows // 2
    core = lax.axis_index("core")
    mine = lax.dynamic_slice_in_dim(weight, core * half, half, axis=0)
    part = lax.all_gather(mine, SHARD, axis=0, tiled=False)
    both = lax.all_gather(part, "core", axis=1, tiled=False)
    return both.reshape(-1, weight.shape[1])


def reduce_rows(partial):
    groups = lax.axis_size(SHARD)
    cols = partial.shape[1]
    blocks = partial.reshape(groups, 2, -1, cols)
    halves = lax.psum_scatter(blocks, "core", scatter_dimension=1, tiled=False)
    owned = lax.psum_scatter(halves, SHARD, scatter_dimension=0, tiled=False)
    owned = lax.psum(owned, "rep_hi")
    return lax.all_gather(owned, "core", axis=0, tiled=True)


def on_device(
    layer_in,
    cotangent,
    seq_lengths,
    norm_gain,
    in_weight,
    conv_weight,
    conv_bias,
    step_bias,
    decay_log,
    skip_gain,
    gate_gain,
    out_weight,
):
    count = layer_in.shape[0]
    groups = lax.axis_size(SHARD)
    segment = segment_ids(seq_lengths[0], count)
    smalls = (norm_gain, conv_weight, conv_bias, step_bias, decay_log, skip_gain, gate_gain)
    flat = jnp.concatenate([a.reshape(-1) for a in smalls])
    flat_all = lax.all_gather(flat, SHARD, axis=0, tiled=False)
    pieces_full = []
    offset = 0
    for a in smalls:
        size = a.size
        block = flat_all[:, offset : offset + size]
        pieces_full.append(block.reshape((groups * a.shape[0],) + a.shape[1:]))
        offset += size
    norm_full, convw_full, convb_full, stepb_full, decay_full, skip_full, gategain_full = (
        pieces_full
    )
    normed_f, norm_back = jax.vjp(norm_input, layer_in, norm_full)
    normed = normed_f.astype(jnp.bfloat16)
    in_whole = gather_rows(in_weight)
    out_whole = gather_rows(out_weight)
    projected = jnp.dot(normed, in_whole, preferred_element_type=jnp.float32)

    def bound_mixer(proj_arg, cw_arg, cb_arg, sb_arg, dl_arg, sk_arg, gg_arg):
        return mixer(proj_arg, segment, cw_arg, cb_arg, sb_arg, dl_arg, sk_arg, gg_arg)

    gated_f, mixer_back = jax.vjp(
        bound_mixer,
        projected,
        convw_full,
        convb_full,
        stepb_full,
        decay_full,
        skip_full,
        gategain_full,
    )
    gated = gated_f.astype(jnp.bfloat16)
    branch_out = jnp.dot(gated, out_whole, preferred_element_type=jnp.float32)
    layer_out = layer_in + branch_out
    cot_low = cotangent.astype(jnp.bfloat16)
    out_owned = reduce_rows(row_product(gated, cot_low))
    gated_grad = back_product(cot_low, out_whole)
    proj_grad, g_convw, g_convb, g_stepb, g_decay, g_skip, g_gategain = mixer_back(gated_grad)
    proj_low = proj_grad.astype(jnp.bfloat16)
    cols = proj_low.shape[1]
    wide = -(-cols // 128) * 128
    proj_wide = jnp.pad(proj_low, ((0, 0), (0, wide - cols)))
    in_owned = reduce_rows(row_product(normed, proj_wide))[:, :cols]
    normed_grad = back_product(proj_low, in_whole)
    back_in, g_norm = norm_back(normed_grad)
    input_grad = cotangent + back_in
    grads = (g_norm, g_convw, g_convb, g_stepb, g_decay, g_skip, g_gategain)
    small_blocks = jnp.concatenate([g.reshape(groups, -1) for g in grads], axis=1)
    small_sum = lax.psum(small_blocks, ALL)
    mine = lax.dynamic_index_in_dim(small_sum, lax.axis_index(SHARD), axis=0, keepdims=False)
    small_final = []
    offset = 0
    for g in grads:
        size = g.size // groups
        small_final.append(
            mine[offset : offset + size].reshape((g.shape[0] // groups,) + g.shape[1:])
        )
        offset += size
    return (
        layer_out,
        input_grad,
        small_final[0],
        in_owned,
        small_final[1],
        small_final[2],
        small_final[3],
        small_final[4],
        small_final[5],
        small_final[6],
        out_owned,
    )


def solution(mesh):
    split = Mesh(
        mesh.devices.reshape(mesh.shape["rep"] // 2, 2, 4, 2),
        ("rep_hi", "core", "shard_0", "shard_1"),
    )
    in_specs = (
        P(REP_SHARD, None),
        P(REP_SHARD, None),
        P(REP_SHARD, None),
        P(SHARD),
        P(SHARD, None),
        P(SHARD, None),
        P(SHARD),
        P(SHARD),
        P(SHARD),
        P(SHARD),
        P(SHARD),
        P(SHARD, None),
    )
    out_specs = (
        P(REP_SHARD, None),
        P(REP_SHARD, None),
        P(SHARD),
        P(SHARD, None),
        P(SHARD, None),
        P(SHARD),
        P(SHARD),
        P(SHARD),
        P(SHARD),
        P(SHARD),
        P(SHARD, None),
    )
    return jax.shard_map(
        on_device, mesh=split, in_specs=in_specs, out_specs=out_specs, check_vma=False
    )
```

profile of v0, /device:TPU:1, one launch (start us, length us, event | category | flops | bytes accessed | tf_op | source)
XLA Modules:
  0.0 826.9 jit_solution(1690237678751658720)
XLA Ops:
  11.3 100.5 %all-gather.16.cloned.1.call-done = bf16[512,4384]{1,0:T(8,128)(2,1)} async-done(((bf16[64,4384]{1,0:T(8,128)(2,1)}), bf16[512,4384]{1,0:T(8,128)(2,1)}) %all-gather.16.cloned.1.call-update) | async-done | bytes 4489232 | tf_op jit(solution)/shard_map/all_gather | solution.py:147
  114.2 26.8 %all-reduce.19 = f32[14688]{0:T(1024)S(1)} all-reduce(f32[14688]{0:T(1024)S(1)} %dynamic-update-slice), channel_id=2, replica_groups=mesh['rep_hi'=8,'core'=2,'shard_0'=4,'shard_1'=2] {'shard_0','shard_1'}, use_global_device_ids=true, to_apply=%add.19 | all-reduce | flops 14688 | bytes 117504
  146.4 21.5 %all-gather.20.cloned.1.call-done = bf16[1024,1024]{1,0:T(8,128)(2,1)} async-done(((bf16[128,1024]{1,0:T(8,128)(2,1)}), bf16[1024,1024]{1,0:T(8,128)(2,1)}) %all-gather.20.cloned.1.call-update) | async-done | bytes 2097168 | tf_op jit(solution)/shard_map/all_gather | solution.py:147
  168.0 25.5 %all-gather.18.cloned.1.call-done = bf16[8,128,4384]{2,1,0:T(8,128)(2,1)} async-done(((bf16[8,64,4384]{2,1,0:T(8,128)(2,1)}), bf16[8,128,4384]{2,1,0:T(8,128)(2,1)}) %all-gather.18.cloned.1.call-update) | async-done | bytes 8978448 | tf_op jit(solution)/shard_map/all_gather | solution.py:148
  193.4 7.5 fusion.74
  204.6 3.7 slice.178
  212.6 7.5 fusion.19
  224.8 9.2 %fusion.24 = f32[256,32,64]{0,2,1:T(8,128)S(1)} fusion(f32[256,32,64]{0,2,1:T(8,128)S(1)} %bitcast.148, f32[256,32,64]{0,2,1:T(8,128)S(1)} %fusion.45, f32[256,256]{1,0:T(8,128)S(1)} %fusion.53, f32[32,256]{1,0:T(8,128)S(1)} %bitcast_add_fusion.2, pred[256,256]{1,0:T(8,128)(4,1)S(1)} %copy-done.39, f32[32]{0:T(128)S(1)} %mul.424, ...), kind=kOutput, calls=%fused_computation.41 | convolution fusion | flops 1619525632 | bytes 6717568 | tf_op jit(solution)/shard_map/jvp(chij,cjhp->cihp)/dot_general | solution.py:129
  234.0 3.1 multiply_reduce_fusion.9
  238.4 14.0 %copy.71 = f32[8,2,128,1024]{3,2,0,1:T(8,128)} copy(f32[8,2,128,1024]{3,2,1,0:T(8,128)S(1)} %bitcast.137) | data formatting | bytes 16777216 | tf_op jit(solution)/shard_map/reshape | solution.py:155
  253.2 4.8 multiply_reduce_fusion.5
  258.1 4.1 multiply_reduce_fusion.6
  262.2 11.4 %fusion.6 = (f32[32,256]{1,0:T(8,128)S(1)}, f32[32,256]{1,0:T(8,128)S(1)}, f32[256,256]{1,0:T(8,128)S(1)}) fusion(f32[256,256]{1,0:T(8,128)S(1)} %copy-done.25, f32[32,256]{1,0:T(8,128)S(1)} %copy-done.43, pred[256,256]{1,0:T(8,128)(4,1)S(1)} %copy-done.40, f32[32,64,256]{2,1,0:T(8,128)S(1)} %bitcast.138, f32[256,32,64]{0,2,1:T(8,128)S(1)} %bitcast.150, ...), kind=kOutput, calls=%fused_computation.7 | convolution fusion | flops 1629929472 | bytes 4915200 | tf_op jit(solution)/shard_map/transpose(jvp(chij,cjhp->cihp))/dot_general | solution.py:129
  275.0 3.2 reduce-window.19
  285.5 3.0 fusion.36
  288.7 9.0 %fusion.25 = (f32[256,32]{0,1:T(8,128)S(1)}, f32[1,256,32,64]{1,3,2,0:T(8,128)S(1)}) fusion(f32[1,256,32,64]{1,3,2,0:T(8,128)} %bitcast.149, f32[256,32]{0,1:T(8,128)} %get-tuple-element.73, f32[32,64,256]{2,1,0:T(8,128)} %bitcast.140, f32[256,256]{1,0:T(8,128)} %copy-done.24, f32[32,256]{1,0:T(8,128)} %copy-done.42, pred[256,256]{1,0:T(8,128)(4,1)} %fusion.50), kind=kOutput, calls=%fused_computation.45 | convolution fusion | flops 1618468864 | bytes 6717440 | tf_op jit(solution)/shard_map/transpose(jvp(chij,cjhp->cihp))/dot_general | solution.py:129
  316.0 6.6 copy.70
  323.4 31.1 %reduce-scatter.5.cloned.1.call-done = f32[8,1,64,4480]{3,2,0,1:T(8,128)} async-done(((f32[8,2,64,4480]{3,2,0,1:T(8,128)}), f32[8,1,64,4480]{3,2,0,1:T(8,128)}) %reduce-scatter.5.cloned.1.call-update) | async-done | bytes 9175056 | tf_op jit(solution)/shard_map/reduce_scatter | solution.py:156
  354.6 94.9 %reduce-scatter.11.cloned.1.call-done = f32[1,128,1024]{2,1,0:T(8,128)} async-done(((f32[8,128,1024]{2,1,0:T(8,128)}), f32[1,128,1024]{2,1,0:T(8,128)}) %reduce-scatter.11.cloned.1.call-update) | async-done | bytes 524304 | tf_op jit(solution)/shard_map/reduce_scatter | solution.py:157
  449.4 186.6 %reduce-scatter.7.cloned.1.call-done = f32[1,64,4480]{2,1,0:T(8,128)} async-done(((f32[8,64,4480]{2,1,0:T(8,128)}), f32[1,64,4480]{2,1,0:T(8,128)}) %reduce-scatter.7.cloned.1.call-update) | async-done | bytes 1146896 | tf_op jit(solution)/shard_map/reduce_scatter | solution.py:157
  636.1 89.9 %all-reduce.23.cloned.1.call-done = (f32[64,4480]{1,0:T(8,128)}, f32[128,1024]{1,0:T(8,128)}) async-done(((f32[64,4480]{1,0:T(8,128)}, f32[128,1024]{1,0:T(8,128)}), (f32[64,4480]{1,0:T(8,128)}, f32[128,1024]{1,0:T(8,128)})) %all-reduce.23.cloned.1.call-update) | async-done | bytes 1671184 | tf_op jit(solution)/shard_map/psum | solution.py:158
  730.8 7.9 multiply_reduce_fusion.10
  738.8 68.5 %psum.21 = f32[8,1836]{1,0:T(8,128)S(1)} all-reduce(f32[8,1836]{1,0:T(8,128)S(1)} %concatenate.35), channel_id=1, replica_groups=mesh['rep_hi'=8,'core'=2,'shard_0'=4,'shard_1'=2] {'rep_hi','core','shar..., use_global_device_ids=true, to_apply=%region_26.27 | all-reduce | flops 14688 | bytes 117504 | tf_op jit(solution)/shard_map/psum | solution.py:228
  815.8 3.2 copy.72
  (278 shorter events, 67.5 us)
Async XLA Ops:
  7.2 104.6 %all-gather.16.cloned.1.call-start = ((), (), s32[]{:S(2)}) async-start(), calls=%async_computation.10 | async-start | bytes 5160960 | tf_op jit(solution)/shard_map/all_gather | solution.py:147
  10.5 157.4 %all-gather.20.cloned.1.call-start = ((), (), s32[]{:S(2)}) async-start(), calls=%async_computation.12 | async-start | bytes 2359296 | tf_op jit(solution)/shard_map/all_gather | solution.py:147
  11.3 100.7 %copy-start.53 = (f32[288,4]{0,1:T(4,128)S(1)}, f32[288,4]{0,1:T(4,128)}, u32[]{:S(2)}) copy-start(f32[288,4]{0,1:T(4,128)} %param.17) | copy-start | bytes 13828
  11.3 182.1 %all-gather.18.cloned.1.call-start = ((), (), s32[]{:S(2)}) async-start(), calls=%async_computation.11 | async-start | bytes 13762560 | tf_op jit(solution)/shard_map/all_gather | solution.py:148
  111.9 141.3 %all-gather.22.cloned.1.call-start = ((), (), s32[]{:S(2)}) async-start(), calls=%async_computation.13 | async-start | bytes 6291456 | tf_op jit(solution)/shard_map/all_gather | solution.py:148
  141.6 59.3 %copy-start.60 = (f32[32]{0:T(128)}, f32[32]{0:T(128)S(1)}, u32[]{:S(2)}) copy-start(f32[32]{0:T(128)S(1)} %neg.39) | copy-start | bytes 388
  145.4 67.1 %copy-start.31 = (f32[2304]{0:T(1024)}, f32[2304]{0:T(1024)S(1)}, u32[]{:S(2)}) copy-start(f32[2304]{0:T(1024)S(1)} %get-tuple-element.53) | copy-start | bytes 27652
  145.4 67.1 %copy-start.33 = (f32[2304]{0:T(1024)}, f32[2304]{0:T(1024)S(1)}, u32[]{:S(2)}) copy-start(f32[2304]{0:T(1024)S(1)} %get-tuple-element.54) | copy-start | bytes 27652
  145.4 67.1 %copy-start.35 = (f32[2304]{0:T(1024)}, f32[2304]{0:T(1024)S(1)}, u32[]{:S(2)}) copy-start(f32[2304]{0:T(1024)S(1)} %get-tuple-element.56) | copy-start | bytes 27652
  145.5 67.1 %copy-start.37 = (f32[2304]{0:T(1024)}, f32[2304]{0:T(1024)S(1)}, u32[]{:S(2)}) copy-start(f32[2304]{0:T(1024)S(1)} %get-tuple-element.55) | copy-start | bytes 27652
  145.6 67.0 %copy-start.54 = (pred[256]{0:T(512)(128)(4,1)}, pred[256]{0:T(512)(128)(4,1)S(1)}, u32[]{:S(2)}) copy-start(pred[256]{0:T(512)(128)(4,1)S(1)} %get-tuple-element.90) | copy-start | bytes 772
  145.6 67.0 %copy-start.56 = (pred[256]{0:T(512)(128)(4,1)}, pred[256]{0:T(512)(128)(4,1)S(1)}, u32[]{:S(2)}) copy-start(pred[256]{0:T(512)(128)(4,1)S(1)} %get-tuple-element.91) | copy-start | bytes 772
  145.6 67.0 %copy-start.58 = (pred[256]{0:T(512)(128)(4,1)}, pred[256]{0:T(512)(128)(4,1)S(1)}, u32[]{:S(2)}) copy-start(pred[256]{0:T(512)(128)(4,1)S(1)} %get-tuple-element.92) | copy-start | bytes 772
  145.6 74.8 %copy-start.48 = (f32[256]{0:T(256)}, f32[256]{0:T(256)S(1)}, u32[]{:S(2)}) copy-start(f32[256]{0:T(256)S(1)} %get-tuple-element.89) | copy-start | bytes 3076
  167.9 154.8 %reduce-scatter.9.cloned.1.call-start = ((), (), s32[]{:S(2)}) async-start(), calls=%async_computation.7 | async-start | bytes 12582912 | tf_op jit(solution)/shard_map/reduce_scatter | solution.py:156
  252.4 102.1 %reduce-scatter.5.cloned.1.call-start = ((), (), s32[]{:S(2)}) async-start(), calls=%async_computation.4 | async-start | bytes 27525120 | tf_op jit(solution)/shard_map/reduce_scatter | solution.py:156
  322.6 126.8 %reduce-scatter.11.cloned.1.call-start = ((), (), s32[]{:S(2)}) async-start(), calls=%async_computation.8 | async-start | bytes 4718592 | tf_op jit(solution)/shard_map/reduce_scatter | solution.py:157
  323.4 312.6 %reduce-scatter.7.cloned.1.call-start = ((), (), s32[]{:S(2)}) async-start(), calls=%async_computation.5 | async-start | bytes 10321920 | tf_op jit(solution)/shard_map/reduce_scatter | solution.py:157
  354.5 372.4 %copy-start.52 = (f32[2048]{0:T(1024)S(1)}, f32[2048]{0:T(1024)}, u32[]{:S(2)}) copy-start(f32[2048]{0:T(1024)} %get-tuple-element.47) | copy-start | bytes 24580
  354.5 371.5 %all-reduce.23.cloned.1.call-start = ((), (), s32[]{:S(2)}) async-start(), calls=%async_computation.14 | async-start | bytes 3342336 | tf_op jit(solution)/shard_map/psum | solution.py:158
  636.0 179.8 %all-gather.14.cloned.1.call-start = ((), (), s32[]{:S(2)}) async-start(), calls=%async_computation.9 | async-start | bytes 1572864 | tf_op jit(solution)/shard_map/all_gather | solution.py:159
  726.0 89.8 %all-gather.12.cloned.1.call-start = ((), (), s32[]{:S(2)}) async-start(), calls=%async_computation.6 | async-start | bytes 3440640 | tf_op jit(solution)/shard_map/all_gather | solution.py:159
  730.8 79.9 %copy-start.51 = (f32[256]{0:T(256)S(1)}, f32[256]{0:T(256)}, u32[]{:S(2)}) copy-start(f32[256]{0:T(256)} %copy-done.50) | copy-start | bytes 3076
  738.8 74.6 %copy-start.47 = (f32[256]{0:T(256)S(1)}, f32[256]{0:T(256)}, u32[]{:S(2)}) copy-start(f32[256]{0:T(256)} %copy-done.46) | copy-start | bytes 3076
  (61 other events, 445.8 us)
Sparse Core Ops, SparseCore 0:
  10.6 101.1 all-gather.15
  114.0 53.8 all-gather.19
  169.6 23.8 all-gather.17
  194.9 17.6 all-gather.21
  252.5 20.8 reduce-scatter.8
  322.8 31.6 reduce-scatter.4
  357.0 92.3 reduce-scatter.10
  452.0 183.9 reduce-scatter.6
  638.8 87.1 all-reduce.22
  727.5 15.0 all-gather.13
  744.3 14.8 all-gather.11
where the time goes:
time: 835 us; the launch traced here: 827 us
  waiting for transfers between devices  551 us (66%)
  blocking collectives  95.2 us (11%)
  local copies, waits for them, and re-layouts  64.2 us (8%)
  matrix products  64 us (8%)
  other arithmetic  35.6 us (4%)
  between operations  16.2 us (2%)
    reduce_scatter x2, waiting for transfers between devices, reduce_rows(): owned = lax.psum_scatter(halves, SHARD, scatter_dimension=0, tiled=False)  281 us
    all_gather x2, waiting for transfers between devices, gather_rows(): part = lax.all_gather(mine, SHARD, axis=0, tiled=False)  122 us
    psum x1, waiting for transfers between devices, reduce_rows(): owned = lax.psum(owned, 'rep_hi')  89.9 us
    psum x1, blocking collectives, on_device(): small_sum = lax.psum(small_blocks, ALL)  68.5 us
    reduce_scatter x2, waiting for transfers between devices, reduce_rows(): halves = lax.psum_scatter(blocks, 'core', scatter_dimension=1, tiled=False)  31.1 us
    dot_general x3, matrix products, mixer(): y_intra = jnp.einsum('chij,cjhp->cihp', mixing, scaled_in, precision=HIGH)  29.5 us
    unnamed x1, blocking collectives  26.8 us
    all_gather x2, waiting for transfers between devices, gather_rows(): both = lax.all_gather(part, 'core', axis=1, tiled=False)  25.5 us
  transfers between devices with their start and end apart: 11, of which 7 were waited for; matrix products, arithmetic and copies ran while one was open for 18% of the time, Pallas kernels for 0%

commit v1 on v0

--- a/solution.py
+++ b/solution.py
@@ -225,7 +225,8 @@
     input_grad = cotangent + back_in
     grads = (g_norm, g_convw, g_convb, g_stepb, g_decay, g_skip, g_gategain)
     small_blocks = jnp.concatenate([g.reshape(groups, -1) for g in grads], axis=1)
-    small_sum = lax.psum(small_blocks, ALL)
+    parts = lax.all_gather(small_blocks, ALL, axis=0, tiled=False)
+    small_sum = parts.sum(axis=0)
     mine = lax.dynamic_index_in_dim(small_sum, lax.axis_index(SHARD), axis=0, keepdims=False)
     small_final = []
     offset = 0

time: 835 us -> 1090 us (1.31)
  waiting for transfers between devices: 551 us -> 872 us
  blocking collectives: 95.2 us -> 26.8 us
    all_gather x0 -> x1, waiting for transfers between devices: none -> 311 us  [on_device(): parts = lax.all_gather(small_blocks, ALL, axis=0, tiled=False)]
    psum x1 -> x0, blocking collectives: 68.5 us -> none  [on_device(): small_sum = lax.psum(small_blocks, ALL)]
    all_gather x2, waiting for transfers between devices: 0.01 us -> 22.7 us  [reduce_rows(): return lax.all_gather(owned, 'core', axis=0, tiled=True)]
    psum x1, waiting for transfers between devices: 89.9 us -> 76.7 us  [reduce_rows(): owned = lax.psum(owned, 'rep_hi')]
  transfers between devices with their start and end apart: 11 -> 12, of which waited for: 7 -> 10; matrix products, arithmetic and copies ran while one was open for 18% -> 14% of each run, Pallas kernels for 0% -> 0%
where the time goes in v1:
time: 1090 us; the launch traced here: 1080 us
  waiting for transfers between devices  872 us (80%)
  local copies, waits for them, and re-layouts  64.8 us (6%)
  matrix products  64 us (6%)
  other arithmetic  39.4 us (4%)
  blocking collectives  26.8 us (2%)
  between operations  16.6 us (2%)
    all_gather x1, waiting for transfers between devices, on_device(): parts = lax.all_gather(small_blocks, ALL, axis=0, tiled=False)  311 us
    reduce_scatter x2, waiting for transfers between devices, reduce_rows(): owned = lax.psum_scatter(halves, SHARD, scatter_dimension=0, tiled=False)  281 us
    all_gather x2, waiting for transfers between devices, gather_rows(): part = lax.all_gather(mine, SHARD, axis=0, tiled=False)  122 us
    psum x1, waiting for transfers between devices, reduce_rows(): owned = lax.psum(owned, 'rep_hi')  76.7 us
    reduce_scatter x2, waiting for transfers between devices, reduce_rows(): halves = lax.psum_scatter(blocks, 'core', scatter_dimension=1, tiled=False)  31.1 us
    dot_general x3, matrix products, mixer(): y_intra = jnp.einsum('chij,cjhp->cihp', mixing, scaled_in, precision=HIGH)  29.5 us
    unnamed x1, blocking collectives  26.8 us
    all_gather x2, waiting for transfers between devices, gather_rows(): both = lax.all_gather(part, 'core', axis=1, tiled=False)  25.5 us
  transfers between devices with their start and end apart: 12, of which 10 were waited for; matrix products, arithmetic and copies ran while one was open for 14% of the time, Pallas kernels for 0%

profile of v1, /device:TPU:1, one launch (start us, length us, event | category | flops | bytes accessed | tf_op | source)
XLA Modules:
  0.0 1084.2 jit_solution(12530968779439841013)
XLA Ops:
  11.3 100.5 %all-gather.18.cloned.1.call-done = bf16[512,4384]{1,0:T(8,128)(2,1)} async-done(((bf16[64,4384]{1,0:T(8,128)(2,1)}), bf16[512,4384]{1,0:T(8,128)(2,1)}) %all-gather.18.cloned.1.call-update) | async-done | bytes 4489232 | tf_op jit(solution)/shard_map/all_gather | solution.py:147
  114.2 26.8 %all-reduce.19 = f32[14688]{0:T(1024)S(1)} all-reduce(f32[14688]{0:T(1024)S(1)} %dynamic-update-slice), channel_id=2, replica_groups=mesh['rep_hi'=8,'core'=2,'shard_0'=4,'shard_1'=2] {'shard_0','shard_1'}, use_global_device_ids=true, to_apply=%add.19 | all-reduce | flops 14688 | bytes 117504
  146.4 21.5 %all-gather.22.cloned.1.call-done = bf16[1024,1024]{1,0:T(8,128)(2,1)} async-done(((bf16[128,1024]{1,0:T(8,128)(2,1)}), bf16[1024,1024]{1,0:T(8,128)(2,1)}) %all-gather.22.cloned.1.call-update) | async-done | bytes 2097168 | tf_op jit(solution)/shard_map/all_gather | solution.py:147
  168.0 25.5 %all-gather.20.cloned.1.call-done = bf16[8,128,4384]{2,1,0:T(8,128)(2,1)} async-done(((bf16[8,64,4384]{2,1,0:T(8,128)(2,1)}), bf16[8,128,4384]{2,1,0:T(8,128)(2,1)}) %all-gather.20.cloned.1.call-update) | async-done | bytes 8978448 | tf_op jit(solution)/shard_map/all_gather | solution.py:148
  193.4 7.5 fusion.74
  204.6 3.7 slice.178
  212.6 7.5 fusion.19
  224.8 9.2 fusion.24
  238.4 14.0 %copy.71 = f32[8,2,128,1024]{3,2,0,1:T(8,128)} copy(f32[8,2,128,1024]{3,2,1,0:T(8,128)S(1)} %bitcast.139) | data formatting | bytes 16777216 | tf_op jit(solution)/shard_map/reshape | solution.py:155
  253.2 4.8 multiply_reduce_fusion.5
  258.1 4.1 multiply_reduce_fusion.6
  262.2 11.4 %fusion.6 = (f32[32,256]{1,0:T(8,128)S(1)}, f32[32,256]{1,0:T(8,128)S(1)}, f32[256,256]{1,0:T(8,128)S(1)}) fusion(f32[256,256]{1,0:T(8,128)S(1)} %copy-done.25, f32[32,256]{1,0:T(8,128)S(1)} %copy-done.43, pred[256,256]{1,0:T(8,128)(4,1)S(1)} %copy-done.40, f32[32,64,256]{2,1,0:T(8,128)S(1)} %bitcast.140, f32[256,32,64]{0,2,1:T(8,128)S(1)} %bitcast.152, ...), kind=kOutput, calls=%fused_computation.8 | convolution fusion | flops 1629929472 | bytes 4915200 | tf_op jit(solution)/shard_map/transpose(jvp(chij,cjhp->cihp))/dot_general | solution.py:129
  274.9 3.2 reduce-window.19
  288.6 9.0 fusion.25
  316.0 6.6 copy.70
  323.4 31.1 %reduce-scatter.5.cloned.1.call-done = f32[8,1,64,4480]{3,2,0,1:T(8,128)} async-done(((f32[8,2,64,4480]{3,2,0,1:T(8,128)}), f32[8,1,64,4480]{3,2,0,1:T(8,128)}) %reduce-scatter.5.cloned.1.call-update) | async-done | bytes 9175056 | tf_op jit(solution)/shard_map/reduce_scatter | solution.py:156
  354.5 94.9 %reduce-scatter.11.cloned.1.call-done = f32[1,128,1024]{2,1,0:T(8,128)} async-done(((f32[8,128,1024]{2,1,0:T(8,128)}), f32[1,128,1024]{2,1,0:T(8,128)}) %reduce-scatter.11.cloned.1.call-update) | async-done | bytes 524304 | tf_op jit(solution)/shard_map/reduce_scatter | solution.py:157
  449.4 186.6 %reduce-scatter.7.cloned.1.call-done = f32[1,64,4480]{2,1,0:T(8,128)} async-done(((f32[8,64,4480]{2,1,0:T(8,128)}), f32[1,64,4480]{2,1,0:T(8,128)}) %reduce-scatter.7.cloned.1.call-update) | async-done | bytes 1146896 | tf_op jit(solution)/shard_map/reduce_scatter | solution.py:157
  640.5 8.0 multiply_reduce_fusion.10
  649.2 76.7 %all-reduce.23.cloned.1.call-done = (f32[64,4480]{1,0:T(8,128)}, f32[128,1024]{1,0:T(8,128)}) async-done(((f32[64,4480]{1,0:T(8,128)}, f32[128,1024]{1,0:T(8,128)}), (f32[64,4480]{1,0:T(8,128)}, f32[128,1024]{1,0:T(8,128)})) %all-reduce.23.cloned.1.call-update) | async-done | bytes 1671184 | tf_op jit(solution)/shard_map/psum | solution.py:158
  731.9 311.2 %all-gather.26.cloned.1.call-done = f32[1024,1836]{1,0:T(8,128)} async-done(((f32[8,1836]{1,0:T(8,128)}), f32[1024,1836]{1,0:T(8,128)}) %all-gather.26.cloned.1.call-update) | async-done | bytes 7520272 | tf_op jit(solution)/shard_map/all_gather | solution.py:228
  1043.1 3.6 bitcast_reduce_fusion
  1050.1 6.3 all-gather.16.cloned.1.call-done
  1056.4 16.4 %all-gather.14.cloned.1.call-done = f32[128,4480]{1,0:T(8,128)} async-done(((f32[64,4480]{1,0:T(8,128)}), f32[128,4480]{1,0:T(8,128)}) %all-gather.14.cloned.1.call-update) | async-done | bytes 2293776 | tf_op jit(solution)/shard_map/all_gather | solution.py:159
  (281 shorter events, 77.8 us)
Async XLA Ops:
  7.2 104.6 %all-gather.18.cloned.1.call-start = ((), (), s32[]{:S(2)}) async-start(), calls=%async_computation.10 | async-start | bytes 5160960 | tf_op jit(solution)/shard_map/all_gather | solution.py:147
  10.5 157.4 %all-gather.22.cloned.1.call-start = ((), (), s32[]{:S(2)}) async-start(), calls=%async_computation.12 | async-start | bytes 2359296 | tf_op jit(solution)/shard_map/all_gather | solution.py:147
  11.3 100.7 %copy-start.53 = (f32[288,4]{0,1:T(4,128)S(1)}, f32[288,4]{0,1:T(4,128)}, u32[]{:S(2)}) copy-start(f32[288,4]{0,1:T(4,128)} %param.17) | copy-start | bytes 13828
  11.3 182.1 %all-gather.20.cloned.1.call-start = ((), (), s32[]{:S(2)}) async-start(), calls=%async_computation.11 | async-start | bytes 13762560 | tf_op jit(solution)/shard_map/all_gather | solution.py:148
  111.9 141.3 %all-gather.24.cloned.1.call-start = ((), (), s32[]{:S(2)}) async-start(), calls=%async_computation.13 | async-start | bytes 6291456 | tf_op jit(solution)/shard_map/all_gather | solution.py:148
  141.6 59.3 %copy-start.60 = (f32[32]{0:T(128)}, f32[32]{0:T(128)S(1)}, u32[]{:S(2)}) copy-start(f32[32]{0:T(128)S(1)} %neg.39) | copy-start | bytes 388
  145.4 67.1 %copy-start.31 = (f32[2304]{0:T(1024)}, f32[2304]{0:T(1024)S(1)}, u32[]{:S(2)}) copy-start(f32[2304]{0:T(1024)S(1)} %get-tuple-element.53) | copy-start | bytes 27652
  145.4 67.1 %copy-start.33 = (f32[2304]{0:T(1024)}, f32[2304]{0:T(1024)S(1)}, u32[]{:S(2)}) copy-start(f32[2304]{0:T(1024)S(1)} %get-tuple-element.54) | copy-start | bytes 27652
  145.4 67.1 %copy-start.35 = (f32[2304]{0:T(1024)}, f32[2304]{0:T(1024)S(1)}, u32[]{:S(2)}) copy-start(f32[2304]{0:T(1024)S(1)} %get-tuple-element.56) | copy-start | bytes 27652
  145.5 67.1 %copy-start.37 = (f32[2304]{0:T(1024)}, f32[2304]{0:T(1024)S(1)}, u32[]{:S(2)}) copy-start(f32[2304]{0:T(1024)S(1)} %get-tuple-element.55) | copy-start | bytes 27652
  145.6 67.0 %copy-start.54 = (pred[256]{0:T(512)(128)(4,1)}, pred[256]{0:T(512)(128)(4,1)S(1)}, u32[]{:S(2)}) copy-start(pred[256]{0:T(512)(128)(4,1)S(1)} %get-tuple-element.90) | copy-start | bytes 772
  145.6 67.0 %copy-start.56 = (pred[256]{0:T(512)(128)(4,1)}, pred[256]{0:T(512)(128)(4,1)S(1)}, u32[]{:S(2)}) copy-start(pred[256]{0:T(512)(128)(4,1)S(1)} %get-tuple-element.91) | copy-start | bytes 772
  145.6 67.0 %copy-start.58 = (pred[256]{0:T(512)(128)(4,1)}, pred[256]{0:T(512)(128)(4,1)S(1)}, u32[]{:S(2)}) copy-start(pred[256]{0:T(512)(128)(4,1)S(1)} %get-tuple-element.92) | copy-start | bytes 772
  145.6 74.8 %copy-start.48 = (f32[256]{0:T(256)}, f32[256]{0:T(256)S(1)}, u32[]{:S(2)}) copy-start(f32[256]{0:T(256)S(1)} %get-tuple-element.89) | copy-start | bytes 3076
  167.9 154.8 %reduce-scatter.9.cloned.1.call-start = ((), (), s32[]{:S(2)}) async-start(), calls=%async_computation.7 | async-start | bytes 12582912 | tf_op jit(solution)/shard_map/reduce_scatter | solution.py:156
  252.4 102.0 %reduce-scatter.5.cloned.1.call-start = ((), (), s32[]{:S(2)}) async-start(), calls=%async_computation.4 | async-start | bytes 27525120 | tf_op jit(solution)/shard_map/reduce_scatter | solution.py:156
  322.6 126.8 %reduce-scatter.11.cloned.1.call-start = ((), (), s32[]{:S(2)}) async-start(), calls=%async_computation.8 | async-start | bytes 4718592 | tf_op jit(solution)/shard_map/reduce_scatter | solution.py:157
  323.4 312.6 %reduce-scatter.7.cloned.1.call-start = ((), (), s32[]{:S(2)}) async-start(), calls=%async_computation.5 | async-start | bytes 10321920 | tf_op jit(solution)/shard_map/reduce_scatter | solution.py:157
  354.4 281.9 %copy-start.52 = (f32[2048]{0:T(1024)S(1)}, f32[2048]{0:T(1024)}, u32[]{:S(2)}) copy-start(f32[2048]{0:T(1024)} %get-tuple-element.47) | copy-start | bytes 24580
  354.5 371.5 %all-reduce.23.cloned.1.call-start = ((), (), s32[]{:S(2)}) async-start(), calls=%async_computation.15 | async-start | bytes 3342336 | tf_op jit(solution)/shard_map/psum | solution.py:158
  636.0 407.1 %all-gather.26.cloned.1.call-start = ((), (), s32[]{:S(2)}) async-start(), calls=%async_computation.14 | async-start | bytes 7925760 | tf_op jit(solution)/shard_map/all_gather | solution.py:228
  640.5 86.1 %copy-start.51 = (f32[256]{0:T(256)S(1)}, f32[256]{0:T(256)}, u32[]{:S(2)}) copy-start(f32[256]{0:T(256)} %copy-done.50) | copy-start | bytes 3076
  649.2 407.2 %all-gather.16.cloned.1.call-start = ((), (), s32[]{:S(2)}) async-start(), calls=%async_computation.9 | async-start | bytes 1572864 | tf_op jit(solution)/shard_map/all_gather | solution.py:159
  726.0 346.8 %all-gather.14.cloned.1.call-start = ((), (), s32[]{:S(2)}) async-start(), calls=%async_computation.6 | async-start | bytes 3440640 | tf_op jit(solution)/shard_map/all_gather | solution.py:159
  (62 other events, 463.5 us)
Sparse Core Ops, SparseCore 0:
  10.6 101.1 all-gather.17
  114.0 53.8 all-gather.21
  169.6 23.8 all-gather.19
  194.9 17.6 all-gather.23
  252.5 20.8 reduce-scatter.8
  322.7 31.6 reduce-scatter.4
  357.0 92.3 reduce-scatter.10
  451.9 183.9 reduce-scatter.6
  638.8 87.1 all-reduce.22
  728.1 314.9 all-gather.25
  1044.7 11.5 all-gather.15
  1057.9 14.8 all-gather.13
